TPU v7x, 32 devices: a whole 2x2x4 slice. The times are simulated.
32 devices in a mesh: grid: 8 (over z, core), vec: 4 (over y, x).
Axes of the slice: x: 2, y: 2, z: 4, core: 2. Of those that a mesh axis runs over, the one named last changes fastest.
Arguments:
- orbitals: bfloat16 [884736, 512], P(('grid', 'vec')), may hold values from -1.296875 to 1.296875
- inverse_panel: bfloat16 [2048, 32], replicated, may hold values from -0.125 to 0.125
- points: int32 [2048], replicated, may hold values from 0 to 884735, as said below
Outputs:
- projected: float32 [2048, 32], P(('grid', 'vec'))
Inputs may be any that keep to these rules, and one draw needn't show every extreme that they name: `points`: distinct cell indices.
All inputs are finite; a program needn't handle non-finite values.
Results may differ from a plain program's by a relative error of at most 0.005.
Values may be sent and summed in bfloat16 or wider, within the bound.
A program may use at most 256 MiB of HBM per device.

v0:
```python
import math

import jax
import jax.numpy as jnp
from jax import lax
from jax.sharding import PartitionSpec as P

NG = 96


SCREEN = 2.25


def wave_tables(count):
    index = lax.iota(jnp.int32, count)
    phase = index[:, None] * index[None, :] % count
    angle = phase.astype(jnp.float32) * (2.0 * math.pi / count)
    return (jnp.cos(angle).astype(jnp.bfloat16), jnp.sin(angle).astype(jnp.bfloat16))


def wavenumber(index, count):
    return jnp.where(index < count // 2, index, index - count).astype(jnp.float32)


def screened(wave_x, wave_y, wave_z):
    squared = (
        wave_x[:, None, None] * wave_x[:, None, None]
        + wave_y[None, :, None] * wave_y[None, :, None]
        + wave_z[None, None, :] * wave_z[None, None, :]
    )
    factor = NG / (2.0 * math.pi) * (NG / (2.0 * math.pi))
    return jnp.where(squared > 0.5, factor / (squared + SCREEN), jnp.float32(0.0))


def mult(data, table, form):
    return jnp.einsum(form, data, table, preferred_element_type=jnp.float32)


def shards(orbitals, inverse_panel, points):
    bf = jnp.bfloat16
    row_count = orbitals.shape[0]
    grid_count = lax.axis_size("grid")
    vec_count = lax.axis_size("vec")
    npoints = points.shape[0]
    offset = (lax.axis_index("grid") * vec_count + lax.axis_index("vec")) * row_count
    local_pos = points - offset
    inside = (local_pos >= 0) & (local_pos < row_count)
    picked = jnp.take(orbitals, jnp.clip(local_pos, 0, row_count - 1), axis=0)
    picked = jnp.where(inside[:, None], picked, jnp.zeros_like(picked)).astype(jnp.float32)
    summed_rows = lax.psum(picked, ("grid", "vec"))
    point_rows = summed_rows.astype(bf)

    def pair_block(block):
        correlation = lax.dot_general(
            block, point_rows, (((1,), (1,)), ((), ())), preferred_element_type=jnp.float32
        )
        return (correlation * correlation).astype(bf)

    pair = lax.map(pair_block, orbitals.reshape(4, row_count // 4, orbitals.shape[1])).reshape(
        row_count, npoints
    )
    fit_cols = lax.dot_general(
        inverse_panel, pair, (((0,), (1,)), ((), ())), preferred_element_type=jnp.float32
    ).astype(bf)
    slab = lax.all_to_all(fit_cols, "vec", split_axis=0, concat_axis=1, tiled=True)
    col_local = slab.shape[0]
    planes = NG // grid_count
    field = slab.reshape(col_local, planes, NG, NG)
    cos_tab, sin_tab = wave_tables(NG)
    z_re = mult(field, cos_tab, "vxyz,zk->vxyk").astype(bf)
    z_im = (-mult(field, sin_tab, "vxyz,zk->vxyk")).astype(bf)
    y_re = (mult(z_re, cos_tab, "vxyz,yk->vxkz") + mult(z_im, sin_tab, "vxyz,yk->vxkz")).astype(bf)
    y_im = (mult(z_im, cos_tab, "vxyz,yk->vxkz") - mult(z_re, sin_tab, "vxyz,yk->vxkz")).astype(bf)
    stacked = jnp.stack([y_re, y_im])
    waves = wavenumber(lax.iota(jnp.int32, NG), NG)
    y_waves = wavenumber(lax.axis_index("grid") * planes + lax.iota(jnp.int32, planes), NG)
    kernel = screened(waves, y_waves, waves)[None]
    piece = lax.all_to_all(stacked, "grid", split_axis=3, concat_axis=2, tiled=True)
    p_re = piece[0]
    p_im = piece[1]
    x_re = mult(p_re, cos_tab, "vxyz,xk->vkyz") + mult(p_im, sin_tab, "vxyz,xk->vkyz")
    x_im = mult(p_im, cos_tab, "vxyz,xk->vkyz") - mult(p_re, sin_tab, "vxyz,xk->vkyz")
    q_re = (x_re * kernel).astype(bf)
    q_im = (x_im * kernel).astype(bf)
    i_re = (mult(q_re, cos_tab, "vxyz,xk->vkyz") - mult(q_im, sin_tab, "vxyz,xk->vkyz")).astype(bf)
    i_im = (mult(q_im, cos_tab, "vxyz,xk->vkyz") + mult(q_re, sin_tab, "vxyz,xk->vkyz")).astype(bf)
    spectrum = lax.all_to_all(
        jnp.stack([i_re, i_im]), "grid", split_axis=2, concat_axis=3, tiled=True
    )
    s_re = spectrum[0]
    s_im = spectrum[1]
    h_re = (mult(s_re, cos_tab, "vxyz,yk->vxkz") - mult(s_im, sin_tab, "vxyz,yk->vxkz")).astype(bf)
    h_im = (mult(s_im, cos_tab, "vxyz,yk->vxkz") + mult(s_re, sin_tab, "vxyz,yk->vxkz")).astype(bf)
    final = mult(h_re, cos_tab, "vxyz,zk->vxyk") - mult(h_im, sin_tab, "vxyz,zk->vxyk")
    potential = (final / float(NG**3)).astype(bf).reshape(col_local, planes * NG * NG)
    pot_rows = lax.all_to_all(potential, "vec", split_axis=1, concat_axis=0, tiled=True)
    scale = 1.0 / math.sqrt(float(NG**3))
    term = lax.dot_general(
        pair, pot_rows, (((0,), (1,)), ((), ())), preferred_element_type=jnp.float32
    )
    partial_block = lax.psum_scatter(
        term * jnp.float32(scale), "grid", scatter_dimension=0, tiled=True
    )
    projected = lax.psum_scatter(partial_block, "vec", scatter_dimension=0, tiled=True)
    return projected


def solution(mesh):
    in_specs = (P(("grid", "vec"), None), P(), P())
    out_specs = P(("grid", "vec"), None)
    return jax.shard_map(shards, mesh=mesh, in_specs=in_specs, out_specs=out_specs, check_vma=False)
```

profile of v0, /device:TPU:0, one launch (start us, length us, event | category | flops | bytes accessed | tf_op | source)
XLA Modules:
  0.0 691.5 jit_solution(2763133241385044677)
XLA Ops:
  8.0 20.3 %gather_fusion = bf16[2048,512]{1,0:T(8,128)(2,1)S(1)} fusion(bf16[27648,512]{1,0:T(8,128)(2,1)} %param.5, s32[2048]{0:T(1024)S(1)} %fusion.73), kind=kCustom, calls=%fused_computation | custom fusion | bytes 4202496 | tf_op jit(solution)/shard_map/jit(_take)/gather | solution.py:48
  28.3 3.4 select_convert_fusion
  31.7 94.7 %all-reduce.1 = bf16[2048,512]{1,0:T(8,128)(2,1)S(1)} all-reduce(f32[2048,512]{1,0:T(8,128)} %select_convert_fusion), channel_id=1, replica_groups=mesh['grid'=8,'vec'=4] {'grid','vec'}, use_global_device_ids=true, to_apply=%region_0.1 | all-reduce | flops 1048576 | bytes 6291456 | tf_op jit(solution)/shard_map/psum | solution.py:50
  126.4 86.1 %while.10 = (s32[]{:T(128)}, bf16[4,6912,2048]{2,1,0:T(8,128)(2,1)}, bf16[4,6912,512]{2,1,0:T(8,128)(2,1)}, bf16[2048,512]{1,0:T(8,128)(2,1)S(1)}, s32[]{:T(128)}) while((s32[]{:T(128)}, bf16[4,6912,2048]{2,1,0:T(8,128)(2,1)}, bf16[4,6912,512]{2,1,0:T(8,128)(2,1)}, bf16[2048,512]{1,0:T(8,128)(2,1)S(1)}, s32[]{:T(128)}) %tuple.28), condition=%wide.region_2.3_spmd, body=%wide.region_1.2_spmd.sunk | while | flops 14523826176 | bytes 37487676 | solution.py:59
  126.4 21.5 %bitcast_dynamic-update-slice_fusion.2 = bf16[4,6912,2048]{2,1,0:T(8,128)(2,1)} fusion(bf16[4,6912,2048]{2,1,0:T(8,128)(2,1)} %get-tuple-element.73, s32[]{:T(128)} %get-tuple-element.72, bf16[2048,512]{1,0:T(8,128)(2,1)S(1)} %get-tuple-element.80, bf16[4,6912,512]{2,1,0:T(8,128)(2,1)} %get-tuple-element.79), kind=kOutput, calls=%fused_computation.2.clone.1 | convolution fusion | flops 14523826176 | bytes 37487616 | tf_op jit(solution)/shard_map/while/body/eval_jaxpr/dot_general | solution.py:54
  147.9 21.5 %bitcast_dynamic-update-slice_fusion.2 = bf16[4,6912,2048]{2,1,0:T(8,128)(2,1)} fusion(bf16[4,6912,2048]{2,1,0:T(8,128)(2,1)} %get-tuple-element.73, s32[]{:T(128)} %get-tuple-element.72, bf16[2048,512]{1,0:T(8,128)(2,1)S(1)} %get-tuple-element.80, bf16[4,6912,512]{2,1,0:T(8,128)(2,1)} %get-tuple-element.79), kind=kOutput, calls=%fused_computation.2.clone.1 | convolution fusion | flops 14523826176 | bytes 37487616 | tf_op jit(solution)/shard_map/while/body/eval_jaxpr/dot_general | solution.py:54
  169.4 21.5 %bitcast_dynamic-update-slice_fusion.2 = bf16[4,6912,2048]{2,1,0:T(8,128)(2,1)} fusion(bf16[4,6912,2048]{2,1,0:T(8,128)(2,1)} %get-tuple-element.73, s32[]{:T(128)} %get-tuple-element.72, bf16[2048,512]{1,0:T(8,128)(2,1)S(1)} %get-tuple-element.80, bf16[4,6912,512]{2,1,0:T(8,128)(2,1)} %get-tuple-element.79), kind=kOutput, calls=%fused_computation.2.clone.1 | convolution fusion | flops 14523826176 | bytes 37487616 | tf_op jit(solution)/shard_map/while/body/eval_jaxpr/dot_general | solution.py:54
  190.9 21.6 %bitcast_dynamic-update-slice_fusion.2 = bf16[4,6912,2048]{2,1,0:T(8,128)(2,1)} fusion(bf16[4,6912,2048]{2,1,0:T(8,128)(2,1)} %get-tuple-element.73, s32[]{:T(128)} %get-tuple-element.72, bf16[2048,512]{1,0:T(8,128)(2,1)S(1)} %get-tuple-element.80, bf16[4,6912,512]{2,1,0:T(8,128)(2,1)} %get-tuple-element.79), kind=kOutput, calls=%fused_computation.2.clone.1 | convolution fusion | flops 14523826176 | bytes 37487616 | tf_op jit(solution)/shard_map/while/body/eval_jaxpr/dot_general | solution.py:54
  212.5 42.6 %fusion.3 = bf16[4,8,27648]{2,1,0:T(8,128)(2,1)S(1)} fusion(bf16[27648,2048]{1,0:T(8,128)(2,1)} %bitcast.3, bf16[2048,32]{0,1:T(8,128)(2,1)S(1)} %copy-done), kind=kOutput, calls=%fused_computation.7 | convolution fusion | flops 3624763392 | bytes 115146752 | tf_op jit(solution)/shard_map/dot_general | solution.py:62
  255.1 23.7 %all_to_all.65 = bf16[4,8,27648]{2,1,0:T(8,128)(2,1)S(1)} all-to-all(bf16[4,8,27648]{2,1,0:T(8,128)(2,1)S(1)} %fusion.3), channel_id=1, replica_groups=mesh['grid'=8,'vec'=4] {'vec'}, dimensions={0} | all-to-all | bytes 3538944 | tf_op jit(solution)/shard_map/all_to_all | solution.py:65
  278.9 2.6 copy.77
  281.5 4.0 reshape.103
  285.5 1.0 convolution_convert_fusion.1
  286.5 1.0 negate_convert_fusion
  287.4 1.0 fusion.56
  288.4 1.0 fusion.54
  289.4 1.0 fusion.4
  290.5 1.0 fusion.5
  291.5 1.1 pad_maximum_fusion
  292.5 5.2 copy.82
  297.7 4.6 all-to-all-start.1
  302.9 104.7 %all-to-all-done.1 = bf16[2,8,12,96,96]{4,1,2,0,3:T(8,128)(2,1)} async-done(((bf16[2,8,12,96,96]{4,1,2,0,3:T(8,128)(2,1)}), bf16[2,8,12,96,96]{4,1,2,0,3:T(8,128)(2,1)}, u32[]{:S(2)}, u32[]{:S(2)}) %all-to-all-start.1) | async-done | bytes 3538976 | tf_op jit(solution)/shard_map/all_to_all | solution.py:78
  407.6 3.6 copy.83
  411.2 0.8 fusion.139
  412.2 2.0 fusion.32
  414.4 2.0 fusion.28
  416.4 2.4 fusion.6
  418.8 1.0 fusion.59
  419.8 2.4 fusion.7
  422.1 1.0 fusion.51
  423.1 1.2 fusion.8
  424.4 1.0 fusion.9
  425.4 1.1 pad_maximum_fusion.1
  426.5 3.0 copy.98
  429.5 107.7 %all_to_all.66 = bf16[2,8,96,12,96]{4,1,3,0,2:T(8,128)(2,1)S(1)} all-to-all(bf16[2,8,96,12,96]{4,1,3,0,2:T(8,128)(2,1)S(1)} %copy.98), channel_id=1, replica_groups=mesh['grid'=8,'vec'=4] {'grid'}, dimensions={2} | all-to-all | bytes 7077888 | tf_op jit(solution)/shard_map/all_to_all | solution.py:87
  537.2 0.8 copy.99
  539.1 3.2 fusion.26
  542.6 1.4 copy-done.2
  543.9 3.1 fusion.20
  547.1 7.1 %fusion.11 = f32[8,12,96,96]{3,2,1,0:T(8,128)} fusion(f32[96,8,12,96]{3,0,2,1:T(8,128)} %fusion.26, bf16[8,12,96,96]{3,0,2,1:T(8,128)(2,1)} %bitcast.130), kind=kOutput, calls=%fused_computation.27 | convolution fusion | flops 341692416 | bytes 8847360 | tf_op jit(solution)/shard_map/vxyz,zk->vxyk/dot_general | solution.py:36
  554.2 5.9 multiply_convert_fusion.1
  560.1 5.0 all_to_all.57
  565.6 24.6 %all_to_all.67 = bf16[8,4,27648]{2,0,1:T(8,128)(2,1)S(1)} all-to-all(bf16[8,4,27648]{2,0,1:T(8,128)(2,1)S(1)} %copy.110), channel_id=1, replica_groups=mesh['grid'=8,'vec'=4] {'vec'}, dimensions={1} | all-to-all | bytes 3538944 | tf_op jit(solution)/shard_map/all_to_all | solution.py:96
  590.2 38.7 %convolution_multiply_fusion = f32[2048,32]{0,1:T(8,128)} fusion(bf16[27648,2048]{1,0:T(8,128)(2,1)} %bitcast.3, bf16[8,4,27648]{2,0,1:T(8,128)(2,1)S(1)} %all_to_all.67), kind=kOutput, calls=%fused_computation.32 | convolution fusion | flops 3623944192 | bytes 115277824 | tf_op jit(solution)/shard_map/dot_general | solution.py:98
  629.0 28.7 %reduce-scatter.5.cloned.1.call-done = f32[256,32]{0,1:T(8,128)} async-done(((f32[2048,32]{0,1:T(8,128)}), f32[256,32]{0,1:T(8,128)}) %reduce-scatter.5.cloned.1.call-update) | async-done | bytes 32784 | tf_op jit(solution)/shard_map/reduce_scatter | solution.py:101
  657.7 1.5 copy.145
  659.2 23.5 %reduce-scatter.7.cloned.1.call-done = f32[64,32]{1,0:T(8,128)} async-done(((f32[256,32]{1,0:T(8,128)}), f32[64,32]{1,0:T(8,128)}) %reduce-scatter.7.cloned.1.call-update) | async-done | bytes 8208
  682.8 1.4 copy.146
  (22 shorter events, 4.2 us)
Async XLA Ops:
  6.5 206.0 %copy-start = (bf16[2048,32]{0,1:T(8,128)(2,1)S(1)}, bf16[2048,32]{0,1:T(8,128)(2,1)}, u32[]{:S(2)}) copy-start(bf16[2048,32]{0,1:T(8,128)(2,1)} %param.6) | copy-start | bytes 393220
  297.7 109.8 %all-to-all-start.1 = ((bf16[2,8,12,96,96]{4,1,2,0,3:T(8,128)(2,1)}), bf16[2,8,12,96,96]{4,1,2,0,3:T(8,128)(2,1)}, u32[]{:S(2)}, u32[]{:S(2)}) async-start(bf16[2,8,12,96,96]{4,1,2,0,3:T(8,128)(2,1)} %copy.82), calls=%async_computation.1 | async-start | bytes 9437184 | tf_op jit(solution)/shard_map/all_to_all | solution.py:78
  302.3 355.4 %reduce-scatter.5.cloned.1.call-start = ((), (), s32[]{:S(2)}) async-start(), calls=%async_computation.6 | async-start | bytes 294912 | tf_op jit(solution)/shard_map/reduce_scatter | solution.py:101
  542.5 1.4 copy-start.2
  590.2 94.0 %copy-start.1 = (bf16[2048,32]{0,1:T(8,128)(2,1)S(1)}, bf16[2048,32]{0,1:T(8,128)(2,1)}, u32[]{:S(2)}) copy-start(bf16[2048,32]{0,1:T(8,128)(2,1)} %param.6) | copy-start | bytes 393220
  628.9 53.8 %reduce-scatter.7.cloned.1.call-start = ((), (), s32[]{:S(2)}) async-start(), calls=%async_computation.7 | async-start | bytes 163840
Sparse Core Ops, SparseCore 0:
  629.1 28.6 reduce-scatter.4
  660.5 22.2 reduce-scatter.6
where the time goes:
time: 697 us; the launch traced here: 691 us
  blocking collectives  251 us (36%)
  matrix products  206 us (30%)
  waiting for transfers between devices  157 us (23%)
  local copies, waits for them, and re-layouts  51.9 us (7%)
  between operations  14.1 us (2%)
  other arithmetic  7.31 us (1%)
    all_to_all x1, blocking collectives, shards(): lax.all_to_all(jnp.stack([i_re, i_im]), 'grid', split_axis=2, concat_axis...  108 us
    all_to_all x1, waiting for transfers between devices, shards(): lax.all_to_all(stacked, 'grid', split_axis=3, concat_axis=2, tiled=True)  105 us
    psum x1, blocking collectives, shards(): summed_rows = lax.psum(picked, ('grid', 'vec'))  94.7 us
    dot_general x4, matrix products, pair_block(): lax.dot_general(block, point_rows, (((1,), (1,)), ((), ())), preferred_el...  86.1 us
    dot_general x1, matrix products, shards(): lax.dot_general(inverse_panel, pair, (((0,), (1,)), ((), ())), preferred_...  42.6 us
    dot_general x1, matrix products, shards(): lax.dot_general(pair, pot_rows, (((0,), (1,)), ((), ())), preferred_eleme...  38.7 us
    dot_general x18, matrix products, mult(): return jnp.einsum(form, data, table, preferred_element_type=jnp.float32)  38.2 us
    reduce_scatter x1, waiting for transfers between devices, shards(): lax.psum_scatter(term * jnp.float32(scale), 'grid', scatter_dimension=0,...  28.7 us
  transfers between devices with their start and end apart: 3, of which 3 were waited for; matrix products, arithmetic and copies ran while one was open for 0% of the time, Pallas kernels for 0%

commit v1 on v0

--- a/solution.py
+++ b/solution.py
@@ -36,6 +36,45 @@
     return jnp.einsum(form, data, table, preferred_element_type=jnp.float32)
 
 
+def transform(re, im, cos_tab, sin_tab, form, sign):
+    out_re = mult(re, cos_tab, form) + sign * mult(im, sin_tab, form)
+    out_im = mult(im, cos_tab, form) - sign * mult(re, sin_tab, form)
+    return out_re, out_im
+
+
+def solve_columns(fit_cols):
+    bf = jnp.bfloat16
+    axes = ("grid", "vec")
+    flat = lax.all_to_all(fit_cols, axes, split_axis=0, concat_axis=1, tiled=True)
+    field = flat.reshape(flat.shape[0], NG, NG, NG)
+    cos_tab, sin_tab = wave_tables(NG)
+    waves = wavenumber(lax.iota(jnp.int32, NG), NG)
+    kernel = screened(waves, waves, waves)[None]
+    a_re = mult(field, cos_tab, "vxyz,zk->vxyk").astype(bf)
+    a_im = (-mult(field, sin_tab, "vxyz,zk->vxyk")).astype(bf)
+    b_re, b_im = transform(a_re, a_im, cos_tab, sin_tab, "vxyz,yk->vxkz", 1.0)
+    b_re, b_im = b_re.astype(bf), b_im.astype(bf)
+    h_re, h_im = transform(b_re, b_im, cos_tab, sin_tab, "vxyz,xk->vkyz", 1.0)
+    q_re, q_im = (h_re * kernel).astype(bf), (h_im * kernel).astype(bf)
+    g_re, g_im = transform(q_re, q_im, cos_tab, sin_tab, "vxyz,xk->vkyz", -1.0)
+    g_re, g_im = g_re.astype(bf), g_im.astype(bf)
+    p_re, p_im = transform(g_re, g_im, cos_tab, sin_tab, "vxyz,yk->vxkz", -1.0)
+    p_re, p_im = p_re.astype(bf), p_im.astype(bf)
+    final = mult(p_re, cos_tab, "vxyz,zk->vxyk") - mult(p_im, sin_tab, "vxyz,zk->vxyk")
+    potential = (final / float(NG**3)).astype(bf).reshape(flat.shape)
+    return lax.all_to_all(potential, axes, split_axis=1, concat_axis=0, tiled=True)
+
+
+def project(pair, pot_rows):
+    scale = 1.0 / math.sqrt(float(NG**3))
+    term = lax.dot_general(
+        pair, pot_rows, (((0,), (1,)), ((), ())), preferred_element_type=jnp.float32
+    )
+    return lax.psum_scatter(
+        term * jnp.float32(scale), ("grid", "vec"), scatter_dimension=0, tiled=True
+    )
+
+
 def shards(orbitals, inverse_panel, points):
     bf = jnp.bfloat16
     row_count = orbitals.shape[0]
@@ -46,9 +85,8 @@
     local_pos = points - offset
     inside = (local_pos >= 0) & (local_pos < row_count)
     picked = jnp.take(orbitals, jnp.clip(local_pos, 0, row_count - 1), axis=0)
-    picked = jnp.where(inside[:, None], picked, jnp.zeros_like(picked)).astype(jnp.float32)
-    summed_rows = lax.psum(picked, ("grid", "vec"))
-    point_rows = summed_rows.astype(bf)
+    picked = jnp.where(inside[:, None], picked, jnp.zeros_like(picked))
+    point_rows = lax.psum(picked, ("grid", "vec"))
 
     def pair_block(block):
         correlation = lax.dot_general(
@@ -62,6 +100,8 @@
     fit_cols = lax.dot_general(
         inverse_panel, pair, (((0,), (1,)), ((), ())), preferred_element_type=jnp.float32
     ).astype(bf)
+    if inverse_panel.shape[1] % (grid_count * vec_count) == 0:
+        return project(pair, solve_columns(fit_cols))
     slab = lax.all_to_all(fit_cols, "vec", split_axis=0, concat_axis=1, tiled=True)
     col_local = slab.shape[0]
     planes = NG // grid_count
@@ -94,15 +134,7 @@
     final = mult(h_re, cos_tab, "vxyz,zk->vxyk") - mult(h_im, sin_tab, "vxyz,zk->vxyk")
     potential = (final / float(NG**3)).astype(bf).reshape(col_local, planes * NG * NG)
     pot_rows = lax.all_to_all(potential, "vec", split_axis=1, concat_axis=0, tiled=True)
-    scale = 1.0 / math.sqrt(float(NG**3))
-    term = lax.dot_general(
-        pair, pot_rows, (((0,), (1,)), ((), ())), preferred_element_type=jnp.float32
-    )
-    partial_block = lax.psum_scatter(
-        term * jnp.float32(scale), "grid", scatter_dimension=0, tiled=True
-    )
-    projected = lax.psum_scatter(partial_block, "vec", scatter_dimension=0, tiled=True)
-    return projected
+    return project(pair, pot_rows)
 
 
 def solution(mesh):

time: 697 us -> 720 us (1.033)
  blocking collectives: 251 us -> 46.9 us
  waiting for transfers between devices: 157 us -> 314 us
  other arithmetic: 7.31 us -> 73 us
    psum x0 -> x1, waiting for transfers between devices: none -> 137 us  [shards(): point_rows = lax.psum(picked, ('grid', 'vec'))]
    unnamed x3, waiting for transfers between devices: 23.6 us -> 135 us
    all_to_all x3 -> x1, blocking collectives: 156 us -> 46.9 us  [solve_columns(): lax.all_to_all(potential, axes, split_axis=1, concat_axis=0, tiled=True)]
    psum x1 -> x0, blocking collectives: 94.7 us -> none  [shards(): summed_rows = lax.psum(picked, ('grid', 'vec'))]
    all_to_all x1, waiting for transfers between devices: 105 us -> 41.5 us  [solve_columns(): lax.all_to_all(fit_cols, axes, split_axis=0, concat_axis=1, tiled=True)]
    all_to_all x0 -> x2, other arithmetic: none -> 36 us  [solve_columns(): lax.all_to_all(fit_cols, axes, split_axis=0, concat_axis=1, tiled=True)]
    unnamed x0 -> x1, other arithmetic: none -> 32.7 us
    reduce_scatter x1 -> x0, waiting for transfers between devices: 28.7 us -> none  [shards(): lax.psum_scatter(term * jnp.float32(scale), 'grid', scatter_dimension=0,...]
where the time goes in v1:
time: 720 us; the launch traced here: 715 us
  waiting for transfers between devices  314 us (44%)
  matrix products  208 us (29%)
  other arithmetic  73 us (10%)
  local copies, waits for them, and re-layouts  56.1 us (8%)
  blocking collectives  46.9 us (7%)
  between operations  13.8 us (2%)
    psum x1, waiting for transfers between devices, shards(): point_rows = lax.psum(picked, ('grid', 'vec'))  137 us
    unnamed x3, waiting for transfers between devices  135 us
    dot_general x4, matrix products, pair_block(): lax.dot_general(block, point_rows, (((1,), (1,)), ((), ())), preferred_el...  85.1 us
    all_to_all x1, blocking collectives, solve_columns(): lax.all_to_all(potential, axes, split_axis=1, concat_axis=0, tiled=True)  46.9 us
    dot_general x18, matrix products, mult(): return jnp.einsum(form, data, table, preferred_element_type=jnp.float32)  43.6 us
    dot_general x1, matrix products, shards(): lax.dot_general(inverse_panel, pair, (((0,), (1,)), ((), ())), preferred_...  42.6 us
    all_to_all x1, waiting for transfers between devices, solve_columns(): lax.all_to_all(fit_cols, axes, split_axis=0, concat_axis=1, tiled=True)  41.5 us
    dot_general x1, matrix products, project(): lax.dot_general(pair, pot_rows, (((0,), (1,)), ((), ())), preferred_eleme...  37 us
  transfers between devices with their start and end apart: 3, of which 3 were waited for; matrix products, arithmetic and copies ran while one was open for 0% of the time, Pallas kernels for 0%

profile of v1, /device:TPU:0, one launch (start us, length us, event | category | flops | bytes accessed | tf_op | source)
XLA Modules:
  0.0 715.1 jit_solution(15143062516928750963)
XLA Ops:
  6.5 0.7 compare_and_fusion.1
  7.3 0.7 fusion.72
  8.0 20.5 %gather_fusion = bf16[2048,512]{1,0:T(8,128)(2,1)S(1)} fusion(bf16[27648,512]{1,0:T(8,128)(2,1)} %param.5, s32[2048]{0:T(1024)S(1)} %fusion.72), kind=kCustom, calls=%fused_computation | custom fusion | bytes 4202496 | tf_op jit(solution)/shard_map/jit(_take)/gather | solution.py:87
  28.5 2.7 select_select_fusion
  31.3 137.5 %all-reduce.2.cloned.1.call-done = bf16[2048,512]{1,0:T(8,128)(2,1)} async-done(((bf16[2048,512]{1,0:T(8,128)(2,1)}), bf16[2048,512]{1,0:T(8,128)(2,1)}) %all-reduce.2.cloned.1.call-update) | async-done | bytes 2097168 | tf_op jit(solution)/shard_map/psum | solution.py:89
  168.8 85.1 %while.10 = (s32[]{:T(128)}, bf16[4,6912,2048]{2,1,0:T(8,128)(2,1)}, bf16[4,6912,512]{2,1,0:T(8,128)(2,1)}, bf16[2048,512]{1,0:T(8,128)(2,1)}, s32[]{:T(128)}) while((s32[]{:T(128)}, bf16[4,6912,2048]{2,1,0:T(8,128)(2,1)}, bf16[4,6912,512]{2,1,0:T(8,128)(2,1)}, bf16[2048,512]{1,0:T(8,128)(2,1)}, s32[]{:T(128)}) %tuple.26), condition=%wide.region_2.3_spmd, body=%wide.region_1.2_spmd.sunk | while | flops 14523826176 | bytes 37487676 | solution.py:97
  168.8 21.4 %bitcast_dynamic-update-slice_fusion.2 = bf16[4,6912,2048]{2,1,0:T(8,128)(2,1)} fusion(bf16[4,6912,2048]{2,1,0:T(8,128)(2,1)} %get-tuple-element.69, s32[]{:T(128)} %get-tuple-element.68, bf16[2048,512]{1,0:T(8,128)(2,1)} %get-tuple-element.76, bf16[4,6912,512]{2,1,0:T(8,128)(2,1)} %get-tuple-element.75), kind=kOutput, calls=%fused_computation.2.clone.1 | convolution fusion | flops 14523826176 | bytes 37487616 | tf_op jit(solution)/shard_map/while/body/eval_jaxpr/dot_general | solution.py:92
  190.1 21.2 %bitcast_dynamic-update-slice_fusion.2 = bf16[4,6912,2048]{2,1,0:T(8,128)(2,1)} fusion(bf16[4,6912,2048]{2,1,0:T(8,128)(2,1)} %get-tuple-element.69, s32[]{:T(128)} %get-tuple-element.68, bf16[2048,512]{1,0:T(8,128)(2,1)} %get-tuple-element.76, bf16[4,6912,512]{2,1,0:T(8,128)(2,1)} %get-tuple-element.75), kind=kOutput, calls=%fused_computation.2.clone.1 | convolution fusion | flops 14523826176 | bytes 37487616 | tf_op jit(solution)/shard_map/while/body/eval_jaxpr/dot_general | solution.py:92
  211.3 21.3 %bitcast_dynamic-update-slice_fusion.2 = bf16[4,6912,2048]{2,1,0:T(8,128)(2,1)} fusion(bf16[4,6912,2048]{2,1,0:T(8,128)(2,1)} %get-tuple-element.69, s32[]{:T(128)} %get-tuple-element.68, bf16[2048,512]{1,0:T(8,128)(2,1)} %get-tuple-element.76, bf16[4,6912,512]{2,1,0:T(8,128)(2,1)} %get-tuple-element.75), kind=kOutput, calls=%fused_computation.2.clone.1 | convolution fusion | flops 14523826176 | bytes 37487616 | tf_op jit(solution)/shard_map/while/body/eval_jaxpr/dot_general | solution.py:92
  232.6 21.2 %bitcast_dynamic-update-slice_fusion.2 = bf16[4,6912,2048]{2,1,0:T(8,128)(2,1)} fusion(bf16[4,6912,2048]{2,1,0:T(8,128)(2,1)} %get-tuple-element.69, s32[]{:T(128)} %get-tuple-element.68, bf16[2048,512]{1,0:T(8,128)(2,1)} %get-tuple-element.76, bf16[4,6912,512]{2,1,0:T(8,128)(2,1)} %get-tuple-element.75), kind=kOutput, calls=%fused_computation.2.clone.1 | convolution fusion | flops 14523826176 | bytes 37487616 | tf_op jit(solution)/shard_map/while/body/eval_jaxpr/dot_general | solution.py:92
  253.9 42.6 %fusion.3 = bf16[32,1,27648]{2,0,1:T(8,128)(2,1)S(1)} fusion(bf16[27648,2048]{1,0:T(8,128)(2,1)} %bitcast.3, bf16[2048,32]{0,1:T(8,128)(2,1)S(1)} %copy-done), kind=kOutput, calls=%fused_computation.7 | convolution fusion | flops 3624763392 | bytes 115146752 | tf_op jit(solution)/shard_map/dot_general | solution.py:100
  296.4 0.5 broadcast.89
  297.0 2.7 reduce.1
  299.6 3.4 reshape.233
  303.0 3.3 all-to-all-start
  306.4 0.0 reduce-scatter.4.cloned.1.call-start
  306.4 0.1 broadcast_add_fusion
  306.5 41.5 %all-to-all-done = bf16[32,2,13824]{2,1,0:T(2,128)(2,1)S(1)} async-done(((bf16[32,2,13824]{2,1,0:T(2,128)(2,1)}), bf16[32,2,13824]{2,1,0:T(2,128)(2,1)S(1)}, u32[]{:S(2)}, u32[]{:S(2)}) %all-to-all-start) | async-done | bytes 1769504 | tf_op jit(solution)/shard_map/all_to_all | solution.py:48
  348.0 6.7 reshape.234
  354.8 33.3 %reduce = bf16[32,27648]{1,0:T(8,128)(2,1)} reduce(bf16[32,1,27648]{2,1,0:T(2,128)(2,1)} %reshape.234, bf16[]{:T(256)} %constant.77), dimensions={1}, to_apply=%all_to_all.23.reduce_sub_computation | reduce | bytes 3538946 | tf_op jit(solution)/shard_map/all_to_all | solution.py:48
  388.1 3.4 reshape.198
  391.5 0.9 negate_convert_fusion
  392.5 0.9 convolution_convert_fusion.1
  393.4 1.0 fusion.51
  394.4 1.0 fusion.55
  395.4 1.0 fusion.7
  396.4 1.2 fusion.28
  397.7 1.0 fusion.6
  398.7 1.2 fusion.32
  399.9 4.6 multiply_convert_fusion.2
  404.5 1.0 fusion.48
  405.5 4.7 multiply_convert_fusion.3
  410.2 1.0 fusion.58
  411.2 1.0 subtract_convert_fusion.1
  412.3 3.3 fusion.20
  415.6 1.0 add_convert_fusion.1
  416.6 3.4 fusion.26
  420.0 7.4 %fusion.9 = f32[96,96,96]{2,1,0:T(8,128)} fusion(f32[96,96,96]{2,0,1:T(8,128)} %fusion.26, bf16[96,96,96]{2,0,1:T(8,128)(2,1)} %copy-done.2), kind=kOutput, calls=%fused_computation.25 | convolution fusion | flops 342577152 | bytes 8847360 | tf_op jit(solution)/shard_map/vxyz,zk->vxyk/dot_general | solution.py:36
  427.4 7.7 %multiply_convert_fusion.1 = bf16[96,96,96]{2,1,0:T(8,128)(2,1)} fusion(f32[96,96,96]{2,1,0:T(8,128)} %fusion.9, f32[96,96,96]{2,0,1:T(8,128)} %fusion.20, bf16[96,96,96]{2,0,1:T(8,128)(2,1)S(1)} %add_convert_fusion.1), kind=kOutput, calls=%fused_computation.12 | convolution fusion | flops 345231360 | bytes 10616832 | tf_op jit(solution)/shard_map/vxyz,zk->vxyk/dot_general | solution.py:36
  435.1 10.2 %all_to_all.27 = bf16[1,32,27648]{2,0,1:T(2,128)(2,1)} reshape(bf16[96,96,96]{2,1,0:T(8,128)(2,1)} %multiply_convert_fusion.1) | data formatting | bytes 3538944 | tf_op jit(solution)/shard_map/all_to_all | solution.py:65
  445.3 32.7 %reduce.2 = bf16[32,27648]{1,0:T(8,128)(2,1)S(1)} reduce(bf16[32,1,27648]{2,1,0:T(2,128)(2,1)} %bitcast.106, bf16[]{:T(256)} %broadcast.89), dimensions={1}, to_apply=%bitcast.84.reduce_sub_computation | reduce | bytes 3538946
  478.1 2.3 reshape.235
  480.3 46.9 %all_to_all.30 = bf16[32,2,13824]{2,1,0:T(2,128)(2,1)S(1)} all-to-all(bf16[32,2,13824]{2,1,0:T(2,128)(2,1)} %reshape.235), channel_id=1, replica_groups=mesh['grid'=8,'vec'=4] {'grid','vec'}, dimensions={0} | all-to-all | bytes 3538944 | tf_op jit(solution)/shard_map/all_to_all | solution.py:65
  527.2 6.3 reshape.236
  533.5 37.0 %convolution_multiply_fusion = f32[2048,32]{0,1:T(8,128)S(1)} fusion(bf16[27648,2048]{1,0:T(8,128)(2,1)} %bitcast.3, bf16[1,32,27648]{2,0,1:T(2,128)(2,1)} %bitcast.108), kind=kOutput, calls=%fused_computation.32 | convolution fusion | flops 3623944192 | bytes 115277824 | tf_op jit(solution)/shard_map/dot_general | solution.py:70
  570.5 1.3 copy.112
  571.9 134.7 %reduce-scatter.4.cloned.1.call-done = f32[64,32]{1,0:T(8,128)} async-done(((f32[2048,32]{1,0:T(8,128)}), f32[64,32]{1,0:T(8,128)}) %reduce-scatter.4.cloned.1.call-update) | async-done | bytes 8208
  706.6 1.4 copy.113
  (11 shorter events, 0.1 us)
Async XLA Ops:
  6.5 247.3 %copy-start = (bf16[2048,32]{0,1:T(8,128)(2,1)S(1)}, bf16[2048,32]{0,1:T(8,128)(2,1)}, u32[]{:S(2)}) copy-start(bf16[2048,32]{0,1:T(8,128)(2,1)} %param.6) | copy-start | bytes 393220
  6.5 162.2 %all-reduce.2.cloned.1.call-start = ((), (), s32[]{:S(2)}) async-start(), calls=%async_computation.3 | async-start | bytes 4194304 | tf_op jit(solution)/shard_map/psum | solution.py:89
  303.0 45.0 %all-to-all-start = ((bf16[32,2,13824]{2,1,0:T(2,128)(2,1)}), bf16[32,2,13824]{2,1,0:T(2,128)(2,1)S(1)}, u32[]{:S(2)}, u32[]{:S(2)}) async-start(bf16[32,2,13824]{2,1,0:T(2,128)(2,1)} %reshape.233), calls=%async_computation | async-start | bytes 3538944 | tf_op jit(solution)/shard_map/all_to_all | solution.py:48
  306.4 400.2 %reduce-scatter.4.cloned.1.call-start = ((), (), s32[]{:S(2)}) async-start(), calls=%async_computation.4 | async-start | bytes 1081344
  412.2 3.3 copy-start.2
  533.5 174.5 %copy-start.1 = (bf16[2048,32]{0,1:T(8,128)(2,1)S(1)}, bf16[2048,32]{0,1:T(8,128)(2,1)}, u32[]{:S(2)}) copy-start(bf16[2048,32]{0,1:T(8,128)(2,1)} %param.6) | copy-start | bytes 393220
Sparse Core Ops, SparseCore 0:
  31.4 137.3 all-reduce.1
  572.0 134.5 reduce-scatter.3

commit v2 on v1

--- a/solution.py
+++ b/solution.py
@@ -3,6 +3,8 @@
 import jax
 import jax.numpy as jnp
 from jax import lax
+from jax.experimental import pallas as pl
+from jax.experimental.pallas import tpu as pltpu
 from jax.sharding import PartitionSpec as P
 
 NG = 96
@@ -36,6 +38,94 @@
     return jnp.einsum(form, data, table, preferred_element_type=jnp.float32)
 
 
+LANES = 128
+
+
+def exchange_kernel(total, x_ref, o_ref, held, send_sem, recv_sem, own_sem):
+    vec_count = lax.axis_size("vec")
+    count = lax.axis_size("grid") * vec_count
+    me = lax.axis_index("grid") * vec_count + lax.axis_index("vec")
+    land = held if total else o_ref
+
+    def place(index):
+        return (index // vec_count, lax.rem(index, vec_count))
+
+    barrier = pltpu.get_barrier_semaphore()
+
+    def greet(step, carry):
+        pl.semaphore_signal(
+            barrier,
+            inc=1,
+            device_id=place(lax.rem(me + step, count)),
+            device_id_type=pl.DeviceIdType.MESH,
+        )
+        return carry
+
+    lax.fori_loop(1, count, greet, 0)
+    own = pltpu.make_async_copy(x_ref.at[me], land.at[me], own_sem)
+    own.start()
+    pl.semaphore_wait(barrier, count - 1)
+
+    def copy(step, source, slot):
+        peer = lax.rem(me + step, count)
+        return pltpu.make_async_remote_copy(
+            src_ref=x_ref.at[source],
+            dst_ref=land.at[slot],
+            send_sem=send_sem.at[step],
+            recv_sem=recv_sem.at[step],
+            device_id=place(peer),
+            device_id_type=pl.DeviceIdType.MESH,
+        )
+
+    def send(step, carry):
+        copy(step, lax.rem(me + step, count), me).start()
+        return carry
+
+    lax.fori_loop(1, count, send, 0)
+    own.wait()
+
+    def receive(step, carry):
+        source = lax.rem(me + count - step, count)
+        copy(step, source, source).wait_recv()
+        return carry
+
+    lax.fori_loop(1, count, receive, 0)
+    if total:
+        o_ref[...] = jnp.sum(held[...], axis=0)
+
+    def drain(step, carry):
+        copy(step, lax.rem(me + step, count), me).wait_send()
+        return carry
+
+    lax.fori_loop(1, count, drain, 0)
+
+
+def exchange(blocks, ident, total=False):
+    count, rows, lanes = blocks.shape
+    shape = (rows, lanes) if total else blocks.shape
+    held_shape = blocks.shape if total else (1, 8, LANES)
+
+    def body(*refs):
+        exchange_kernel(total, *refs)
+
+    return pl.pallas_call(
+        body,
+        out_shape=jax.ShapeDtypeStruct(shape, blocks.dtype),
+        in_specs=[pl.BlockSpec(memory_space=pltpu.VMEM)],
+        out_specs=pl.BlockSpec(memory_space=pltpu.VMEM),
+        scratch_shapes=[
+            pltpu.VMEM(held_shape, blocks.dtype),
+            pltpu.SemaphoreType.DMA((count,)),
+            pltpu.SemaphoreType.DMA((count,)),
+            pltpu.SemaphoreType.DMA(()),
+        ],
+        compiler_params=pltpu.CompilerParams(
+            collective_id=ident, has_side_effects=True, vmem_limit_bytes=32 << 20
+        ),
+        name="exchange_total" if total else "exchange_blocks",
+    )(blocks)
+
+
 def transform(re, im, cos_tab, sin_tab, form, sign):
     out_re = mult(re, cos_tab, form) + sign * mult(im, sin_tab, form)
     out_im = mult(im, cos_tab, form) - sign * mult(re, sin_tab, form)
@@ -44,9 +134,10 @@
 
 def solve_columns(fit_cols):
     bf = jnp.bfloat16
-    axes = ("grid", "vec")
-    flat = lax.all_to_all(fit_cols, axes, split_axis=0, concat_axis=1, tiled=True)
-    field = flat.reshape(flat.shape[0], NG, NG, NG)
+    count = fit_cols.shape[0]
+    rows = fit_cols.shape[1]
+    flat = exchange(fit_cols.reshape(count, rows // LANES, LANES), 1)
+    field = flat.reshape(1, NG, NG, NG)
     cos_tab, sin_tab = wave_tables(NG)
     waves = wavenumber(lax.iota(jnp.int32, NG), NG)
     kernel = screened(waves, waves, waves)[None]
@@ -62,7 +153,7 @@
     p_re, p_im = p_re.astype(bf), p_im.astype(bf)
     final = mult(p_re, cos_tab, "vxyz,zk->vxyk") - mult(p_im, sin_tab, "vxyz,zk->vxyk")
     potential = (final / float(NG**3)).astype(bf).reshape(flat.shape)
-    return lax.all_to_all(potential, axes, split_axis=1, concat_axis=0, tiled=True)
+    return exchange(potential, 2).reshape(count, rows)
 
 
 def project(pair, pot_rows):
@@ -70,9 +161,15 @@
     term = lax.dot_general(
         pair, pot_rows, (((0,), (1,)), ((), ())), preferred_element_type=jnp.float32
     )
-    return lax.psum_scatter(
-        term * jnp.float32(scale), ("grid", "vec"), scatter_dimension=0, tiled=True
-    )
+    term = term * jnp.float32(scale)
+    npoints, cols = term.shape
+    count = lax.axis_size("grid") * lax.axis_size("vec")
+    share = npoints // count
+    if share * cols % LANES == 0:
+        blocks = term.reshape(count, share * cols // LANES, LANES)
+        return exchange(blocks, 3, True).reshape(share, cols)
+    partial_block = lax.psum_scatter(term, "grid", scatter_dimension=0, tiled=True)
+    return lax.psum_scatter(partial_block, "vec", scatter_dimension=0, tiled=True)
 
 
 def shards(orbitals, inverse_panel, points):
@@ -85,8 +182,9 @@
     local_pos = points - offset
     inside = (local_pos >= 0) & (local_pos < row_count)
     picked = jnp.take(orbitals, jnp.clip(local_pos, 0, row_count - 1), axis=0)
-    picked = jnp.where(inside[:, None], picked, jnp.zeros_like(picked))
-    point_rows = lax.psum(picked, ("grid", "vec"))
+    picked = jnp.where(inside[:, None], picked, jnp.zeros_like(picked)).astype(jnp.float32)
+    summed_rows = lax.psum(picked, ("grid", "vec"))
+    point_rows = summed_rows.astype(bf)
 
     def pair_block(block):
         correlation = lax.dot_general(
@@ -100,7 +198,7 @@
     fit_cols = lax.dot_general(
         inverse_panel, pair, (((0,), (1,)), ((), ())), preferred_element_type=jnp.float32
     ).astype(bf)
-    if inverse_panel.shape[1] % (grid_count * vec_count) == 0:
+    if inverse_panel.shape[1] == grid_count * vec_count and row_count % LANES == 0:
         return project(pair, solve_columns(fit_cols))
     slab = lax.all_to_all(fit_cols, "vec", split_axis=0, concat_axis=1, tiled=True)
     col_local = slab.shape[0]

time: 720 us -> 448 us (0.62)
  waiting for transfers between devices: 314 us -> 0 us
  Pallas kernels: 0 us -> 97.7 us
  other arithmetic: 73 us -> 4.99 us
  blocking collectives: 46.9 us -> 95 us
  local copies, waits for them, and re-layouts: 56.1 us -> 33 us
  between operations: 13.8 us -> 0.48 us
    psum x1 -> x0, waiting for transfers between devices: 137 us -> none  [shards(): point_rows = lax.psum(picked, ('grid', 'vec'))]
    unnamed x3 -> x0, waiting for transfers between devices: 135 us -> none
    pallas_call x0 -> x3, Pallas kernels: none -> 97.7 us  [exchange(): pl.pallas_call(body, out_shape=jax.ShapeDtypeStruct(shape, blocks.dtype),...]
    psum x0 -> x1, blocking collectives: none -> 95 us  [shards(): summed_rows = lax.psum(picked, ('grid', 'vec'))]
    all_to_all x1 -> x0, blocking collectives: 46.9 us -> none  [solve_columns(): lax.all_to_all(potential, axes, split_axis=1, concat_axis=0, tiled=True)]
    all_to_all x1 -> x0, waiting for transfers between devices: 41.5 us -> none  [solve_columns(): lax.all_to_all(fit_cols, axes, split_axis=0, concat_axis=1, tiled=True)]
    all_to_all x2 -> x0, other arithmetic: 36 us -> none  [solve_columns(): lax.all_to_all(fit_cols, axes, split_axis=0, concat_axis=1, tiled=True)]
    unnamed x1 -> x0, other arithmetic: 32.7 us -> none
  transfers between devices with their start and end apart: 3 -> 0, of which waited for: 3 -> 0; matrix products, arithmetic and copies ran while one was open for 0% -> 0% of each run, Pallas kernels for 0% -> 0%
where the time goes in v2:
time: 448 us; the launch traced here: 443 us
  matrix products  212 us (47%)
  Pallas kernels  97.7 us (22%)
  blocking collectives  95 us (21%)
  local copies, waits for them, and re-layouts  33 us (7%)
  other arithmetic  4.99 us (1%)
    pallas_call x3, Pallas kernels, exchange(): pl.pallas_call(body, out_shape=jax.ShapeDtypeStruct(shape, blocks.dtype),...  97.7 us
    psum x1, blocking collectives, shards(): summed_rows = lax.psum(picked, ('grid', 'vec'))  95 us
    dot_general x4, matrix products, pair_block(): lax.dot_general(block, point_rows, (((1,), (1,)), ((), ())), preferred_el...  86.1 us
    dot_general x18, matrix products, mult(): return jnp.einsum(form, data, table, preferred_element_type=jnp.float32)  45.3 us
    dot_general x1, matrix products, shards(): lax.dot_general(inverse_panel, pair, (((0,), (1,)), ((), ())), preferred_...  42.6 us
    dot_general x1, matrix products, project(): lax.dot_general(pair, pot_rows, (((0,), (1,)), ((), ())), preferred_eleme...  38 us
    gather x1, local copies, waits for them, and re-layouts, shards(): picked = jnp.take(orbitals, jnp.clip(local_pos, 0, row_count - 1), axis=0)  20.3 us

profile of v2, /device:TPU:0, one launch (start us, length us, event | category | flops | bytes accessed | tf_op | source)
XLA Modules:
  0.0 443.2 jit_solution(16269613565554483688)
XLA Ops:
  0.0 0.0 copy-start
  0.0 0.7 compare_and_fusion.1
  0.7 0.7 fusion.72
  1.5 20.3 %gather_fusion = bf16[2048,512]{1,0:T(8,128)(2,1)S(1)} fusion(bf16[27648,512]{1,0:T(8,128)(2,1)} %param.5, s32[2048]{0:T(1024)S(1)} %fusion.72), kind=kCustom, calls=%fused_computation | custom fusion | bytes 4202496 | tf_op jit(solution)/shard_map/jit(_take)/gather | solution.py:184
  21.7 3.5 select_convert_fusion
  25.2 95.0 %all-reduce.1 = bf16[2048,512]{1,0:T(8,128)(2,1)S(1)} all-reduce(f32[2048,512]{1,0:T(8,128)} %select_convert_fusion), channel_id=1, replica_groups=mesh['grid'=8,'vec'=4] {'grid','vec'}, use_global_device_ids=true, to_apply=%region_0.1 | all-reduce | flops 1048576 | bytes 6291456 | tf_op jit(solution)/shard_map/psum | solution.py:186
  120.3 86.1 %while.10 = (s32[]{:T(128)}, bf16[4,6912,2048]{2,1,0:T(8,128)(2,1)}, bf16[4,6912,512]{2,1,0:T(8,128)(2,1)}, bf16[2048,512]{1,0:T(8,128)(2,1)S(1)}, s32[]{:T(128)}) while((s32[]{:T(128)}, bf16[4,6912,2048]{2,1,0:T(8,128)(2,1)}, bf16[4,6912,512]{2,1,0:T(8,128)(2,1)}, bf16[2048,512]{1,0:T(8,128)(2,1)S(1)}, s32[]{:T(128)}) %tuple.22), condition=%wide.region_2.3_spmd, body=%wide.region_1.2_spmd.sunk | while | flops 14523826176 | bytes 37487676 | solution.py:195
  120.3 21.5 %bitcast_dynamic-update-slice_fusion.2 = bf16[4,6912,2048]{2,1,0:T(8,128)(2,1)} fusion(bf16[4,6912,2048]{2,1,0:T(8,128)(2,1)} %get-tuple-element.69, s32[]{:T(128)} %get-tuple-element.68, bf16[2048,512]{1,0:T(8,128)(2,1)S(1)} %get-tuple-element.76, bf16[4,6912,512]{2,1,0:T(8,128)(2,1)} %get-tuple-element.75), kind=kOutput, calls=%fused_computation.2.clone.1 | convolution fusion | flops 14523826176 | bytes 37487616 | tf_op jit(solution)/shard_map/while/body/eval_jaxpr/dot_general | solution.py:190
  141.8 21.5 %bitcast_dynamic-update-slice_fusion.2 = bf16[4,6912,2048]{2,1,0:T(8,128)(2,1)} fusion(bf16[4,6912,2048]{2,1,0:T(8,128)(2,1)} %get-tuple-element.69, s32[]{:T(128)} %get-tuple-element.68, bf16[2048,512]{1,0:T(8,128)(2,1)S(1)} %get-tuple-element.76, bf16[4,6912,512]{2,1,0:T(8,128)(2,1)} %get-tuple-element.75), kind=kOutput, calls=%fused_computation.2.clone.1 | convolution fusion | flops 14523826176 | bytes 37487616 | tf_op jit(solution)/shard_map/while/body/eval_jaxpr/dot_general | solution.py:190
  163.2 21.5 %bitcast_dynamic-update-slice_fusion.2 = bf16[4,6912,2048]{2,1,0:T(8,128)(2,1)} fusion(bf16[4,6912,2048]{2,1,0:T(8,128)(2,1)} %get-tuple-element.69, s32[]{:T(128)} %get-tuple-element.68, bf16[2048,512]{1,0:T(8,128)(2,1)S(1)} %get-tuple-element.76, bf16[4,6912,512]{2,1,0:T(8,128)(2,1)} %get-tuple-element.75), kind=kOutput, calls=%fused_computation.2.clone.1 | convolution fusion | flops 14523826176 | bytes 37487616 | tf_op jit(solution)/shard_map/while/body/eval_jaxpr/dot_general | solution.py:190
  184.7 21.6 %bitcast_dynamic-update-slice_fusion.2 = bf16[4,6912,2048]{2,1,0:T(8,128)(2,1)} fusion(bf16[4,6912,2048]{2,1,0:T(8,128)(2,1)} %get-tuple-element.69, s32[]{:T(128)} %get-tuple-element.68, bf16[2048,512]{1,0:T(8,128)(2,1)S(1)} %get-tuple-element.76, bf16[4,6912,512]{2,1,0:T(8,128)(2,1)} %get-tuple-element.75), kind=kOutput, calls=%fused_computation.2.clone.1 | convolution fusion | flops 14523826176 | bytes 37487616 | tf_op jit(solution)/shard_map/while/body/eval_jaxpr/dot_general | solution.py:190
  206.3 0.0 copy-done
  206.3 42.6 %fusion.39 = bf16[4,8,216,128]{3,1,2,0:T(8,128)(2,1)S(1)} fusion(bf16[27648,2048]{1,0:T(8,128)(2,1)} %bitcast.3, bf16[2048,32]{0,1:T(8,128)(2,1)S(1)} %copy-done), kind=kOutput, calls=%fused_computation.48 | convolution fusion | flops 3624763392 | bytes 115146752 | tf_op jit(solution)/shard_map/dot_general | solution.py:198
  249.0 0.2 copy.88
  249.2 32.8 %exchange_blocks.2 = bf16[32,216,128]{2,1,0:T(8,128)(2,1)S(1)} custom-call(bf16[32,216,128]{2,1,0:T(8,128)(2,1)S(1)} %bitcast.105), custom_call_target="tpu_custom_call" | custom-call | tf_op jit(solution)/shard_map/exchange_blocks/pallas_call | solution.py:111
  282.0 3.0 reshape.199
  285.0 2.6 negate_convert_fusion
  287.6 0.0 copy-start.4
  287.6 1.0 fusion.51
  288.7 0.6 copy-done.4
  289.3 0.9 convolution_convert_fusion.1
  290.2 1.0 fusion.6
  291.3 1.2 fusion.27
  292.5 1.0 fusion.55
  293.5 1.0 fusion.5
  294.5 0.1 broadcast_add_fusion
  294.6 4.6 %multiply_convert_fusion.2 = bf16[96,96,96]{2,0,1:T(8,128)(2,1)S(1)} fusion(f32[96,96,96]{2,0,1:T(8,128)S(1)} %fusion.27, f32[96]{0:T(128)S(1)} %fusion.74, f32[96,96]{0,1:T(8,128)S(1)} %broadcast_add_fusion, bf16[96,96,96]{2,1,0:T(8,128)(2,1)S(1)} %fusion.5), kind=kOutput, calls=%fused_computation.16 | convolution fusion | flops 177039360 | bytes 7115136 | tf_op jit(solution)/shard_map/vxyz,xk->vkyz/dot_general | solution.py:38
  299.2 1.0 fusion.48
  300.2 1.2 fusion.31
  301.4 4.8 %multiply_convert_fusion.3 = bf16[96,96,96]{2,0,1:T(8,128)(2,1)S(1)} fusion(f32[96,96,96]{2,0,1:T(8,128)S(1)} %fusion.31, f32[96]{0:T(128)S(1)} %fusion.74, f32[96,96]{0,1:T(8,128)S(1)} %broadcast_add_fusion, bf16[96,96,96]{2,1,0:T(8,128)(2,1)S(1)} %fusion.6), kind=kOutput, calls=%fused_computation.17 | convolution fusion | flops 177039360 | bytes 7115136 | tf_op jit(solution)/shard_map/vxyz,xk->vkyz/dot_general | solution.py:38
  306.2 1.0 subtract_convert_fusion.1
  307.2 0.0 copy-start.3
  307.2 3.3 fusion.19
  310.5 1.0 fusion.58
  311.5 1.0 add_convert_fusion.1
  312.5 3.4 fusion.25
  315.9 7.4 %fusion.8 = f32[96,96,96]{2,1,0:T(8,128)} fusion(f32[96,96,96]{2,0,1:T(8,128)} %fusion.25, bf16[96,96,96]{2,0,1:T(8,128)(2,1)} %copy-done.3), kind=kOutput, calls=%fused_computation.24 | convolution fusion | flops 342577152 | bytes 8847360 | tf_op jit(solution)/shard_map/vxyz,zk->vxyk/dot_general | solution.py:38
  323.4 7.7 %multiply_convert_fusion.1 = bf16[96,96,96]{2,1,0:T(8,128)(2,1)} fusion(f32[96,96,96]{2,1,0:T(8,128)} %fusion.8, f32[96,96,96]{2,0,1:T(8,128)} %fusion.19, bf16[96,96,96]{2,0,1:T(8,128)(2,1)S(1)} %add_convert_fusion.1), kind=kOutput, calls=%fused_computation.11 | convolution fusion | flops 345231360 | bytes 10616832 | tf_op jit(solution)/shard_map/vxyz,zk->vxyk/dot_general | solution.py:38
  331.1 6.0 %reshape.204.refs_0_ = bf16[32,216,128]{2,1,0:T(8,128)(2,1)} reshape(bf16[96,96,96]{2,1,0:T(8,128)(2,1)} %multiply_convert_fusion.1) | data formatting | bytes 3538944 | tf_op jit(solution)/shard_map/reshape | solution.py:155
  337.1 1.5 copy-done.2
  338.6 44.5 %exchange_blocks.3 = bf16[32,216,128]{2,1,0:T(8,128)(2,1)S(1)} custom-call(bf16[32,216,128]{2,1,0:T(8,128)(2,1)S(1)} %copy-done.2), custom_call_target="tpu_custom_call" | custom-call | tf_op jit(solution)/shard_map/exchange_blocks/pallas_call | solution.py:111
  383.1 0.0 copy-start.1
  383.1 38.0 %convolution_multiply_fusion = f32[2048,32]{0,1:T(8,128)S(1)} fusion(bf16[27648,2048]{1,0:T(8,128)(2,1)} %bitcast.3, bf16[4,8,216,128]{3,2,1,0:T(8,128)(2,1)S(1)} %bitcast.104), kind=kOutput, calls=%fused_computation.31 | convolution fusion | flops 3623944192 | bytes 115277824 | tf_op jit(solution)/shard_map/dot_general | solution.py:161
  421.2 0.3 copy.54
  421.5 0.3 reshape.206.refs_0_
  421.8 20.4 %exchange_total.1 = f32[16,128]{1,0:T(8,128)S(1)} custom-call(f32[32,16,128]{2,1,0:T(8,128)S(1)} %reshape.206.refs_0_), custom_call_target="tpu_custom_call" | custom-call | tf_op jit(solution)/shard_map/exchange_total/pallas_call | solution.py:111
  442.2 0.1 reshape.207
  442.2 0.7 copy.55
  (5 shorter events, 0.0 us)
Async XLA Ops:
  0.0 206.3 %copy-start = (bf16[2048,32]{0,1:T(8,128)(2,1)S(1)}, bf16[2048,32]{0,1:T(8,128)(2,1)}, u32[]{:S(2)}) copy-start(bf16[2048,32]{0,1:T(8,128)(2,1)} %param.6) | copy-start | bytes 393220
  287.6 1.7 copy-start.4
  307.2 3.3 copy-start.3
  337.1 1.5 copy-start.2
  383.1 59.8 %copy-start.1 = (bf16[2048,32]{0,1:T(8,128)(2,1)S(1)}, bf16[2048,32]{0,1:T(8,128)(2,1)}, u32[]{:S(2)}) copy-start(bf16[2048,32]{0,1:T(8,128)(2,1)} %param.6) | copy-start | bytes 393220

commit v3 on v2

--- a/solution.py
+++ b/solution.py
@@ -41,14 +41,25 @@
 LANES = 128
 
 
-def exchange_kernel(total, x_ref, o_ref, held, send_sem, recv_sem, own_sem):
-    vec_count = lax.axis_size("vec")
-    count = lax.axis_size("grid") * vec_count
-    me = lax.axis_index("grid") * vec_count + lax.axis_index("vec")
+def exchange_kernel(axes, total, gather, x_ref, o_ref, held, send_sem, recv_sem, own_sem):
+    if len(axes) == 2:
+        vec_count = lax.axis_size("vec")
+        count = lax.axis_size("grid") * vec_count
+        me = lax.axis_index("grid") * vec_count + lax.axis_index("vec")
+    else:
+        count = lax.axis_size(axes[0])
+        me = lax.axis_index(axes[0])
     land = held if total else o_ref
 
     def place(index):
-        return (index // vec_count, lax.rem(index, vec_count))
+        if len(axes) == 2:
+            return (index // vec_count, lax.rem(index, vec_count))
+        if axes[0] == "grid":
+            return (index, lax.axis_index("vec"))
+        return (lax.axis_index("grid"), index)
+
+    def part(index):
+        return x_ref if gather else x_ref.at[index]
 
     barrier = pltpu.get_barrier_semaphore()
 
@@ -62,14 +73,14 @@
         return carry
 
     lax.fori_loop(1, count, greet, 0)
-    own = pltpu.make_async_copy(x_ref.at[me], land.at[me], own_sem)
+    own = pltpu.make_async_copy(part(me), land.at[me], own_sem)
     own.start()
     pl.semaphore_wait(barrier, count - 1)
 
     def copy(step, source, slot):
         peer = lax.rem(me + step, count)
         return pltpu.make_async_remote_copy(
-            src_ref=x_ref.at[source],
+            src_ref=part(source),
             dst_ref=land.at[slot],
             send_sem=send_sem.at[step],
             recv_sem=recv_sem.at[step],
@@ -91,7 +102,7 @@
 
     lax.fori_loop(1, count, receive, 0)
     if total:
-        o_ref[...] = jnp.sum(held[...], axis=0)
+        o_ref[...] = jnp.sum(held[...].astype(jnp.float32), axis=0).astype(o_ref.dtype)
 
     def drain(step, carry):
         copy(step, lax.rem(me + step, count), me).wait_send()
@@ -100,13 +111,16 @@
     lax.fori_loop(1, count, drain, 0)
 
 
-def exchange(blocks, ident, total=False):
-    count, rows, lanes = blocks.shape
-    shape = (rows, lanes) if total else blocks.shape
+def exchange(blocks, ident, total=False, axes=("grid", "vec"), gather=False):
+    rows, lanes = blocks.shape[-2:]
+    count = 1
+    for axis in axes:
+        count *= lax.axis_size(axis)
+    shape = (rows, lanes) if total else (count, rows, lanes)
     held_shape = blocks.shape if total else (1, 8, LANES)
 
     def body(*refs):
-        exchange_kernel(total, *refs)
+        exchange_kernel(axes, total, gather, *refs)
 
     return pl.pallas_call(
         body,
@@ -122,8 +136,25 @@
         compiler_params=pltpu.CompilerParams(
             collective_id=ident, has_side_effects=True, vmem_limit_bytes=32 << 20
         ),
-        name="exchange_total" if total else "exchange_blocks",
+        name="exchange_total" if total else "exchange_gather" if gather else "exchange_blocks",
     )(blocks)
+
+
+def share_rows(picked, grid_count, vec_count):
+    npoints, norb = picked.shape
+    if npoints % (grid_count * vec_count * 16) != 0:
+        return lax.psum(picked.astype(jnp.float32), ("grid", "vec")).astype(picked.dtype)
+    mine = exchange(
+        picked.reshape(vec_count, npoints // vec_count, norb), 4, total=True, axes=("vec",)
+    )
+    mine = exchange(
+        mine.reshape(grid_count, npoints // vec_count // grid_count, norb),
+        5,
+        total=True,
+        axes=("grid",),
+    )
+    block = exchange(mine, 6, axes=("grid",), gather=True).reshape(npoints // vec_count, norb)
+    return exchange(block, 7, axes=("vec",), gather=True).reshape(npoints, norb)
 
 
 def transform(re, im, cos_tab, sin_tab, form, sign):
@@ -182,9 +213,8 @@
     local_pos = points - offset
     inside = (local_pos >= 0) & (local_pos < row_count)
     picked = jnp.take(orbitals, jnp.clip(local_pos, 0, row_count - 1), axis=0)
-    picked = jnp.where(inside[:, None], picked, jnp.zeros_like(picked)).astype(jnp.float32)
-    summed_rows = lax.psum(picked, ("grid", "vec"))
-    point_rows = summed_rows.astype(bf)
+    picked = jnp.where(inside[:, None], picked, jnp.zeros_like(picked))
+    point_rows = share_rows(picked, grid_count, vec_count)
 
     def pair_block(block):
         correlation = lax.dot_general(

time: 448 us -> 437 us (0.975)
  blocking collectives: 95 us -> 0 us
  Pallas kernels: 97.7 us -> 184 us
    psum x1 -> x0, blocking collectives: 95 us -> none  [shards(): summed_rows = lax.psum(picked, ('grid', 'vec'))]
    pallas_call x3 -> x7, Pallas kernels: 97.7 us -> 184 us  [exchange(): pl.pallas_call(body, out_shape=jax.ShapeDtypeStruct(shape, blocks.dtype),...]
where the time goes in v3:
time: 437 us; the launch traced here: 432 us
  matrix products  212 us (49%)
  Pallas kernels  184 us (42%)
  local copies, waits for them, and re-layouts  33.5 us (8%)
    pallas_call x7, Pallas kernels, exchange(): pl.pallas_call(body, out_shape=jax.ShapeDtypeStruct(shape, blocks.dtype),...  184 us
    dot_general x4, matrix products, pair_block(): lax.dot_general(block, point_rows, (((1,), (1,)), ((), ())), preferred_el...  86.1 us
    dot_general x18, matrix products, mult(): return jnp.einsum(form, data, table, preferred_element_type=jnp.float32)  45.3 us
    dot_general x1, matrix products, shards(): lax.dot_general(inverse_panel, pair, (((0,), (1,)), ((), ())), preferred_...  42.6 us
    dot_general x1, matrix products, project(): lax.dot_general(pair, pot_rows, (((0,), (1,)), ((), ())), preferred_eleme...  38 us
    gather x1, local copies, waits for them, and re-layouts, shards(): picked = jnp.take(orbitals, jnp.clip(local_pos, 0, row_count - 1), axis=0)  20.8 us

profile of v3, /device:TPU:0, one launch (start us, length us, event | category | flops | bytes accessed | tf_op | source)
XLA Modules:
  0.0 432.3 jit_solution(10535705733758545811)
XLA Ops:
  0.0 0.7 compare_and_fusion.1
  0.8 0.7 fusion.72
  1.5 20.8 %gather_fusion = bf16[2048,512]{1,0:T(8,128)(2,1)S(1)} fusion(bf16[27648,512]{1,0:T(8,128)(2,1)} %param.5, s32[2048]{0:T(1024)S(1)} %fusion.72), kind=kCustom, calls=%fused_computation | custom fusion | bytes 4202496 | tf_op jit(solution)/shard_map/jit(_take)/gather | solution.py:215
  22.3 0.9 select_select_fusion.refs_0_
  23.2 27.8 %exchange_total.3 = bf16[512,512]{1,0:T(8,128)(2,1)S(1)} custom-call(bf16[4,512,512]{2,1,0:T(8,128)(2,1)S(1)} %select_select_fusion.refs_0_), custom_call_target="tpu_custom_call" | custom-call | tf_op jit(solution)/shard_map/exchange_total/pallas_call | solution.py:125
  51.1 12.8 %exchange_total.4.refs_0_ = bf16[64,512]{1,0:T(8,128)(2,1)S(1)} custom-call(bf16[8,64,512]{2,1,0:T(8,128)(2,1)S(1)} %bitcast.110), custom_call_target="tpu_custom_call" | custom-call | tf_op jit(solution)/shard_map/exchange_total/pallas_call | solution.py:125
  63.9 14.9 %exchange_gather.2 = bf16[8,64,512]{2,1,0:T(8,128)(2,1)S(1)} custom-call(bf16[64,512]{1,0:T(8,128)(2,1)S(1)} %exchange_total.4.refs_0_), custom_call_target="tpu_custom_call" | custom-call | tf_op jit(solution)/shard_map/exchange_gather/pallas_call | solution.py:125
  78.8 26.9 %exchange_gather.3 = bf16[4,512,512]{2,1,0:T(8,128)(2,1)S(1)} custom-call(bf16[512,512]{1,0:T(8,128)(2,1)S(1)} %bitcast.111), custom_call_target="tpu_custom_call" | custom-call | tf_op jit(solution)/shard_map/exchange_gather/pallas_call | solution.py:125
  105.7 86.1 %while.10 = (s32[]{:T(128)}, bf16[4,6912,2048]{2,1,0:T(8,128)(2,1)}, bf16[4,6912,512]{2,1,0:T(8,128)(2,1)}, bf16[2048,512]{1,0:T(8,128)(2,1)S(1)}, s32[]{:T(128)}) while((s32[]{:T(128)}, bf16[4,6912,2048]{2,1,0:T(8,128)(2,1)}, bf16[4,6912,512]{2,1,0:T(8,128)(2,1)}, bf16[2048,512]{1,0:T(8,128)(2,1)S(1)}, s32[]{:T(128)}) %tuple.23), condition=%wide.region_1.2_spmd, body=%wide.region_0.1_spmd.sunk | while | flops 14523826176 | bytes 37487676 | solution.py:225
  105.7 21.5 %bitcast_dynamic-update-slice_fusion.2 = bf16[4,6912,2048]{2,1,0:T(8,128)(2,1)} fusion(bf16[4,6912,2048]{2,1,0:T(8,128)(2,1)} %get-tuple-element.69, s32[]{:T(128)} %get-tuple-element.68, bf16[2048,512]{1,0:T(8,128)(2,1)S(1)} %get-tuple-element.76, bf16[4,6912,512]{2,1,0:T(8,128)(2,1)} %get-tuple-element.75), kind=kOutput, calls=%fused_computation.2.clone.1 | convolution fusion | flops 14523826176 | bytes 37487616 | tf_op jit(solution)/shard_map/while/body/eval_jaxpr/dot_general | solution.py:220
  127.2 21.4 %bitcast_dynamic-update-slice_fusion.2 = bf16[4,6912,2048]{2,1,0:T(8,128)(2,1)} fusion(bf16[4,6912,2048]{2,1,0:T(8,128)(2,1)} %get-tuple-element.69, s32[]{:T(128)} %get-tuple-element.68, bf16[2048,512]{1,0:T(8,128)(2,1)S(1)} %get-tuple-element.76, bf16[4,6912,512]{2,1,0:T(8,128)(2,1)} %get-tuple-element.75), kind=kOutput, calls=%fused_computation.2.clone.1 | convolution fusion | flops 14523826176 | bytes 37487616 | tf_op jit(solution)/shard_map/while/body/eval_jaxpr/dot_general | solution.py:220
  148.7 21.5 %bitcast_dynamic-update-slice_fusion.2 = bf16[4,6912,2048]{2,1,0:T(8,128)(2,1)} fusion(bf16[4,6912,2048]{2,1,0:T(8,128)(2,1)} %get-tuple-element.69, s32[]{:T(128)} %get-tuple-element.68, bf16[2048,512]{1,0:T(8,128)(2,1)S(1)} %get-tuple-element.76, bf16[4,6912,512]{2,1,0:T(8,128)(2,1)} %get-tuple-element.75), kind=kOutput, calls=%fused_computation.2.clone.1 | convolution fusion | flops 14523826176 | bytes 37487616 | tf_op jit(solution)/shard_map/while/body/eval_jaxpr/dot_general | solution.py:220
  170.2 21.6 %bitcast_dynamic-update-slice_fusion.2 = bf16[4,6912,2048]{2,1,0:T(8,128)(2,1)} fusion(bf16[4,6912,2048]{2,1,0:T(8,128)(2,1)} %get-tuple-element.69, s32[]{:T(128)} %get-tuple-element.68, bf16[2048,512]{1,0:T(8,128)(2,1)S(1)} %get-tuple-element.76, bf16[4,6912,512]{2,1,0:T(8,128)(2,1)} %get-tuple-element.75), kind=kOutput, calls=%fused_computation.2.clone.1 | convolution fusion | flops 14523826176 | bytes 37487616 | tf_op jit(solution)/shard_map/while/body/eval_jaxpr/dot_general | solution.py:220
  191.8 0.0 copy-done
  191.8 42.6 %fusion.39 = bf16[4,8,216,128]{3,1,2,0:T(8,128)(2,1)S(1)} fusion(bf16[27648,2048]{1,0:T(8,128)(2,1)} %bitcast.7, bf16[2048,32]{0,1:T(8,128)(2,1)S(1)} %copy-done), kind=kOutput, calls=%fused_computation.48 | convolution fusion | flops 3624763392 | bytes 115146752 | tf_op jit(solution)/shard_map/dot_general | solution.py:228
  234.5 0.2 copy.88
  234.7 36.7 %exchange_blocks.2 = bf16[32,216,128]{2,1,0:T(8,128)(2,1)S(1)} custom-call(bf16[32,216,128]{2,1,0:T(8,128)(2,1)S(1)} %bitcast.109), custom_call_target="tpu_custom_call" | custom-call | tf_op jit(solution)/shard_map/exchange_blocks/pallas_call | solution.py:125
  271.4 3.0 reshape.223
  274.4 2.6 negate_convert_fusion
  277.0 1.0 fusion.51
  278.0 0.6 copy-done.4
  278.7 0.9 convolution_convert_fusion.1
  279.6 1.0 fusion.6
  280.6 1.2 fusion.27
  281.8 1.0 fusion.55
  282.9 1.0 fusion.5
  283.9 0.1 broadcast_add_fusion
  284.0 4.6 %multiply_convert_fusion.2 = bf16[96,96,96]{2,0,1:T(8,128)(2,1)S(1)} fusion(f32[96,96,96]{2,0,1:T(8,128)S(1)} %fusion.27, f32[96]{0:T(128)S(1)} %fusion.74, f32[96,96]{0,1:T(8,128)S(1)} %broadcast_add_fusion, bf16[96,96,96]{2,1,0:T(8,128)(2,1)S(1)} %fusion.5), kind=kOutput, calls=%fused_computation.16 | convolution fusion | flops 177039360 | bytes 7115136 | tf_op jit(solution)/shard_map/vxyz,xk->vkyz/dot_general | solution.py:38
  288.6 1.0 fusion.48
  289.6 1.2 fusion.31
  290.8 4.8 %multiply_convert_fusion.3 = bf16[96,96,96]{2,0,1:T(8,128)(2,1)S(1)} fusion(f32[96,96,96]{2,0,1:T(8,128)S(1)} %fusion.31, f32[96]{0:T(128)S(1)} %fusion.74, f32[96,96]{0,1:T(8,128)S(1)} %broadcast_add_fusion, bf16[96,96,96]{2,1,0:T(8,128)(2,1)S(1)} %fusion.6), kind=kOutput, calls=%fused_computation.17 | convolution fusion | flops 177039360 | bytes 7115136 | tf_op jit(solution)/shard_map/vxyz,xk->vkyz/dot_general | solution.py:38
  295.5 1.0 subtract_convert_fusion.1
  296.6 3.3 fusion.19
  299.9 1.0 fusion.58
  300.9 1.0 add_convert_fusion.1
  301.9 3.4 fusion.25
  305.3 7.4 %fusion.8 = f32[96,96,96]{2,1,0:T(8,128)} fusion(f32[96,96,96]{2,0,1:T(8,128)} %fusion.25, bf16[96,96,96]{2,0,1:T(8,128)(2,1)} %copy-done.3), kind=kOutput, calls=%fused_computation.24 | convolution fusion | flops 342577152 | bytes 8847360 | tf_op jit(solution)/shard_map/vxyz,zk->vxyk/dot_general | solution.py:38
  312.7 7.7 %multiply_convert_fusion.1 = bf16[96,96,96]{2,1,0:T(8,128)(2,1)} fusion(f32[96,96,96]{2,1,0:T(8,128)} %fusion.8, f32[96,96,96]{2,0,1:T(8,128)} %fusion.19, bf16[96,96,96]{2,0,1:T(8,128)(2,1)S(1)} %add_convert_fusion.1), kind=kOutput, calls=%fused_computation.11 | convolution fusion | flops 345231360 | bytes 10616832 | tf_op jit(solution)/shard_map/vxyz,zk->vxyk/dot_general | solution.py:38
  320.5 6.0 %reshape.228.refs_0_ = bf16[32,216,128]{2,1,0:T(8,128)(2,1)} reshape(bf16[96,96,96]{2,1,0:T(8,128)(2,1)} %multiply_convert_fusion.1) | data formatting | bytes 3538944 | tf_op jit(solution)/shard_map/reshape | solution.py:186
  326.5 1.5 copy-done.2
  327.9 44.2 %exchange_blocks.3 = bf16[32,216,128]{2,1,0:T(8,128)(2,1)S(1)} custom-call(bf16[32,216,128]{2,1,0:T(8,128)(2,1)S(1)} %copy-done.2), custom_call_target="tpu_custom_call" | custom-call | tf_op jit(solution)/shard_map/exchange_blocks/pallas_call | solution.py:125
  372.2 0.0 copy-start.1
  372.2 38.0 %convolution_multiply_fusion = f32[2048,32]{0,1:T(8,128)S(1)} fusion(bf16[27648,2048]{1,0:T(8,128)(2,1)} %bitcast.7, bf16[4,8,216,128]{3,2,1,0:T(8,128)(2,1)S(1)} %bitcast.108), kind=kOutput, calls=%fused_computation.31 | convolution fusion | flops 3623944192 | bytes 115277824 | tf_op jit(solution)/shard_map/dot_general | solution.py:192
  410.2 0.3 copy.54
  410.6 0.3 reshape.230.refs_0_
  410.9 20.4 %exchange_total.5 = f32[16,128]{1,0:T(8,128)S(1)} custom-call(f32[32,16,128]{2,1,0:T(8,128)S(1)} %reshape.230.refs_0_), custom_call_target="tpu_custom_call" | custom-call | tf_op jit(solution)/shard_map/exchange_total/pallas_call | solution.py:125
  431.2 0.1 reshape.231
  431.3 0.7 copy.55
  (10 shorter events, 0.0 us)
Async XLA Ops:
  0.0 191.8 %copy-start = (bf16[2048,32]{0,1:T(8,128)(2,1)S(1)}, bf16[2048,32]{0,1:T(8,128)(2,1)}, u32[]{:S(2)}) copy-start(bf16[2048,32]{0,1:T(8,128)(2,1)} %param.6) | copy-start | bytes 393220
  277.0 1.7 copy-start.4
  296.6 3.3 copy-start.3
  326.5 1.5 copy-start.2
  372.2 59.8 %copy-start.1 = (bf16[2048,32]{0,1:T(8,128)(2,1)S(1)}, bf16[2048,32]{0,1:T(8,128)(2,1)}, u32[]{:S(2)}) copy-start(bf16[2048,32]{0,1:T(8,128)(2,1)} %param.6) | copy-start | bytes 393220
